TPU v7x, 32 devices: a whole 2x2x4 slice. The times are simulated.
32 devices in a mesh: fsdp: 2 (over x), context: 4 (over y, core), tensor: 4 (over z).
Axes of the slice: x: 2, y: 2, z: 4, core: 2. Of those that a mesh axis runs over, the one named last changes fastest.
Arguments:
- tokens: bfloat16 [2, 2048, 1024], P('fsdp', 'context'), may hold values from -6 to 6
- cotangent: bfloat16 [2, 2048, 1024], P('fsdp', 'context'), may hold values from -6 to 6
- lengths: int32 [2, 4], P('fsdp'), may hold values from 1 to 1024, 2048 in all within a row
- w_in: bfloat16 [3, 1024, 1024], P(None, 'fsdp', 'tensor'), may hold values from -0.1875 to 0.1875
- w_out: bfloat16 [1024, 1024], P('tensor', 'fsdp'), may hold values from -0.1875 to 0.1875
- w_gate_up: bfloat16 [2, 1024, 4608], P(None, 'fsdp', 'tensor'), may hold values from -0.1875 to 0.1875
- w_down: bfloat16 [4608, 1024], P('tensor', 'fsdp'), may hold values from -0.1875 to 0.1875
- norm_gains: bfloat16 [2, 1024], P(None, 'fsdp'), may hold values from 0.5 to 1.5
- conv_kernel: bfloat16 [3, 1024], P(None, 'tensor'), may hold values from -3 to 3
Outputs:
- block_out: float32 [2, 2048, 1024], P('fsdp', 'context')
- grad_tokens: float32 [2, 2048, 1024], P('fsdp', 'context')
- grad_w_in: float32 [3, 1024, 1024], P(None, 'fsdp', 'tensor')
- grad_w_out: float32 [1024, 1024], P('tensor', 'fsdp')
- grad_w_gate_up: float32 [2, 1024, 4608], P(None, 'fsdp', 'tensor')
- grad_w_down: float32 [4608, 1024], P('tensor', 'fsdp')
- grad_norm_gains: float32 [2, 1024], P(None, 'fsdp')
- grad_conv_kernel: float32 [3, 1024], P(None, 'tensor')
Inputs may be any that keep to these rules, and one draw needn't show every extreme that they name: `lengths`: each row of 2048 tokens is a pack of 4 whole documents, in order; some document of every row has 1024 tokens.
All inputs are finite; a program needn't handle non-finite values.
Results may differ from a plain program's by a relative error of at most 0.0088.
Values may be sent and summed in bfloat16 or wider, within the bound.
No kernel may reach another device: no remote copies, remote signals or barrier semaphores. Data moves between devices by JAX's collectives and lax.ppermute only.
A program may use at most 128 MiB of HBM per device.

v0:
```python
import jax
import jax.numpy as jnp
from jax import lax
from jax.sharding import PartitionSpec as P

norm_eps = 1e-05


def shifted(block, axis, distance):
    devices = range(lax.axis_size(axis))
    route = [(i - distance, i) for i in devices if i - distance in devices]
    return lax.ppermute(block, axis, route)


def matmul_plain(matrix_one, matrix_two):
    return jnp.dot(matrix_one, matrix_two, preferred_element_type=jnp.float32)


def matmul_right(matrix_one, matrix_two):
    return lax.dot_general(
        matrix_one, matrix_two, (((1,), (1,)), ((), ())), preferred_element_type=jnp.float32
    )


def matmul_left(matrix_one, matrix_two):
    return lax.dot_general(
        matrix_one, matrix_two, (((0,), (0,)), ((), ())), preferred_element_type=jnp.float32
    )


def norm_forward(values):
    inv_root = lax.rsqrt(jnp.mean(values * values, axis=-1, keepdims=True) + norm_eps)
    return (values * inv_root, inv_root)


def norm_backward(normed, inv_root, gain_row, grad_out):
    grad_normed = grad_out * gain_row
    inner_mean = jnp.mean(grad_normed * normed, axis=-1, keepdims=True)
    return (inv_root * (grad_normed - normed * inner_mean), jnp.sum(grad_out * normed, axis=0))


def keep_masks(position, lengths_row):
    starts = jnp.cumsum(lengths_row) - lengths_row
    doc_start = jnp.max(jnp.where(starts[None, :] <= position[:, None], starts[None, :], 0), axis=1)
    keep_one = (position - 1 >= doc_start).astype(jnp.float32)[:, None]
    keep_two = (position - 2 >= doc_start).astype(jnp.float32)[:, None]
    return (keep_one, keep_two)


def local(tokens, cotangent, lengths, w_in, w_out, w_gate_up, w_down, norm_gains, conv_kernel):
    block_rows = tokens.shape[1]
    position = lax.axis_index("context") * block_rows + jnp.arange(block_rows + 2, dtype=jnp.int32)
    keep_one_ext, keep_two_ext = keep_masks(position, lengths[0])
    keep_one = keep_one_ext[:block_rows]
    keep_two = keep_two_ext[:block_rows]
    full_in, full_out, full_gate_up, full_down, full_gains = (
        lax.all_gather(w_in, "fsdp", axis=1, tiled=True),
        lax.all_gather(w_out, "fsdp", axis=1, tiled=True),
        lax.all_gather(w_gate_up, "fsdp", axis=1, tiled=True),
        lax.all_gather(w_down, "fsdp", axis=1, tiled=True),
        lax.all_gather(norm_gains, "fsdp", axis=1, tiled=True),
    )
    inputs = tokens[0].astype(jnp.float32)
    gain_first = full_gains[0].astype(jnp.float32)
    gain_second = full_gains[1].astype(jnp.float32)
    kernel_taps = conv_kernel.astype(jnp.float32)
    normed_one, root_one = norm_forward(inputs)
    hidden_one = (normed_one * gain_first).astype(jnp.bfloat16)
    b_part = matmul_plain(hidden_one, full_in[0])
    c_part = matmul_plain(hidden_one, full_in[1])
    x_part = matmul_plain(hidden_one, full_in[2])
    mixed = b_part * x_part
    rim_rows = shifted(mixed[-2:], "context", 1)
    extended = jnp.concatenate([rim_rows, mixed], axis=0)
    back_one = extended[1:-1] * keep_one
    back_two = extended[:-2] * keep_two
    conv_value = kernel_taps[2] * mixed + kernel_taps[1] * back_one + kernel_taps[0] * back_two
    gated = (c_part * conv_value).astype(jnp.bfloat16)
    first_sum = inputs + lax.psum(matmul_plain(gated, full_out), "tensor")
    normed_two, root_two = norm_forward(first_sum)
    hidden_two = (normed_two * gain_second).astype(jnp.bfloat16)
    gate_value = matmul_plain(hidden_two, full_gate_up[0])
    up_value = matmul_plain(hidden_two, full_gate_up[1])
    sigmoid_gate = jax.nn.sigmoid(gate_value)
    silu_gate = gate_value * sigmoid_gate
    act_value = (silu_gate * up_value).astype(jnp.bfloat16)
    output_rows = first_sum + lax.psum(matmul_plain(act_value, full_down), "tensor")
    full_in, full_out, full_gate_up, full_down, full_gains = (
        lax.all_gather(w_in, "fsdp", axis=1, tiled=True),
        lax.all_gather(w_out, "fsdp", axis=1, tiled=True),
        lax.all_gather(w_gate_up, "fsdp", axis=1, tiled=True),
        lax.all_gather(w_down, "fsdp", axis=1, tiled=True),
        lax.all_gather(norm_gains, "fsdp", axis=1, tiled=True),
    )
    cot_rows = cotangent[0]
    grad_act = matmul_right(cot_rows, full_down)
    grad_gate = (
        grad_act * up_value * sigmoid_gate * (1.0 + gate_value * (1.0 - sigmoid_gate))
    ).astype(jnp.bfloat16)
    grad_up = (grad_act * silu_gate).astype(jnp.bfloat16)
    grad_h2 = lax.psum(
        matmul_right(grad_gate, full_gate_up[0]) + matmul_right(grad_up, full_gate_up[1]), "tensor"
    )
    back_second, grad_gain_two = norm_backward(normed_two, root_two, gain_second, grad_h2)
    grad_first = cot_rows.astype(jnp.float32) + back_second
    grad_first_b = grad_first.astype(jnp.bfloat16)
    grad_gated = matmul_right(grad_first_b, full_out)
    grad_conv = grad_gated * c_part
    next_rows = shifted(grad_conv[:2], "context", -1)
    ahead = jnp.concatenate([grad_conv, next_rows], axis=0)
    ahead_one = ahead[1 : block_rows + 1] * keep_one_ext[1 : block_rows + 1]
    ahead_two = ahead[2:] * keep_two_ext[2:]
    grad_mixed = (
        kernel_taps[2] * grad_conv + kernel_taps[1] * ahead_one + kernel_taps[0] * ahead_two
    )
    grad_kernel = jnp.stack(
        [
            jnp.sum(grad_conv * back_two, axis=0),
            jnp.sum(grad_conv * back_one, axis=0),
            jnp.sum(grad_conv * mixed, axis=0),
        ]
    )
    grad_b = (grad_mixed * x_part).astype(jnp.bfloat16)
    grad_c = (grad_gated * conv_value).astype(jnp.bfloat16)
    grad_x = (grad_mixed * b_part).astype(jnp.bfloat16)
    local_h1 = (
        matmul_right(grad_b, full_in[0])
        + matmul_right(grad_c, full_in[1])
        + matmul_right(grad_x, full_in[2])
    )
    grad_h1 = lax.psum(local_h1, "tensor")
    back_first, grad_gain_one = norm_backward(normed_one, root_one, gain_first, grad_h1)
    grad_inputs = grad_first + back_first
    term_in = jnp.stack(
        [
            matmul_left(hidden_one, grad_b),
            matmul_left(hidden_one, grad_c),
            matmul_left(hidden_one, grad_x),
        ]
    )
    term_out = matmul_left(gated, grad_first_b)
    term_gate_up = jnp.stack([matmul_left(hidden_two, grad_gate), matmul_left(hidden_two, grad_up)])
    term_down = matmul_left(act_value, cot_rows)
    term_gains = jnp.stack([grad_gain_one, grad_gain_two])
    pieces = (
        lax.psum_scatter(term_in, "fsdp", scatter_dimension=1, tiled=True),
        lax.psum_scatter(term_out, "fsdp", scatter_dimension=1, tiled=True),
        lax.psum_scatter(term_gate_up, "fsdp", scatter_dimension=1, tiled=True),
        lax.psum_scatter(term_down, "fsdp", scatter_dimension=1, tiled=True),
        lax.psum_scatter(term_gains, "fsdp", scatter_dimension=1, tiled=True),
    )
    reduced = lax.psum((pieces[0], pieces[1], pieces[2], pieces[3], pieces[4]), "context")
    kernel_total = lax.psum(grad_kernel, ("fsdp", "context"))
    return (
        output_rows[None],
        grad_inputs[None],
        reduced[0],
        reduced[1],
        reduced[2],
        reduced[3],
        reduced[4],
        kernel_total,
    )


def solution(mesh):
    placed = (
        P("fsdp", "context", None),
        P("fsdp", "context", None),
        P("fsdp", None),
        P(None, "fsdp", "tensor"),
        P("tensor", "fsdp"),
        P(None, "fsdp", "tensor"),
        P("tensor", "fsdp"),
        P(None, "fsdp"),
        P(None, "tensor"),
    )
    return jax.shard_map(
        local,
        mesh=mesh,
        in_specs=placed,
        out_specs=(
            P("fsdp", "context", None),
            P("fsdp", "context", None),
            P(None, "fsdp", "tensor"),
            P("tensor", "fsdp"),
            P(None, "fsdp", "tensor"),
            P("tensor", "fsdp"),
            P(None, "fsdp"),
            P(None, "tensor"),
        ),
        check_vma=False,
    )
```

profile of v0, /device:TPU:0, one launch (start us, length us, event | category | flops | bytes accessed | tf_op | source)
XLA Modules:
  0.0 958.6 jit_solution(321070914398784171)
XLA Ops:
  9.4 5.5 all_gather.19
  15.0 1.6 fusion.15
  17.5 21.9 %all-gather.4.cloned.1.call-done = bf16[3,1024,256]{2,1,0:T(8,128)(2,1)} async-done(((bf16[3,512,256]{2,1,0:T(8,128)(2,1)}), bf16[3,1024,256]{2,1,0:T(8,128)(2,1)}) %all-gather.4.cloned.1.call-update) | async-done | bytes 1572880 | tf_op jit(solution)/shard_map/all_gather | solution.py:57
  39.5 2.0 fusion.46
  41.5 1.3 fusion.60
  42.8 1.6 collective-permute-start
  44.4 8.9 all_gather.21
  53.3 1.6 multiply_convert_fusion.7
  55.6 1.8 fusion.61
  58.7 84.5 %all-reduce.7.cloned.1.call-done = f32[512,1024]{1,0:T(8,128)} async-done(((f32[512,1024]{1,0:T(8,128)}), f32[512,1024]{1,0:T(8,128)}) %all-reduce.7.cloned.1.call-update) | async-done | bytes 2097168 | tf_op jit(solution)/shard_map/psum | solution.py:79
  143.2 1.9 multiply_reduce_fusion.2
  145.1 1.3 multiply_convert_fusion.3
  146.4 60.0 %all-gather.6.cloned.1.call-done = bf16[2,1024,1152]{2,1,0:T(8,128)(2,1)} async-done(((bf16[2,512,1152]{2,1,0:T(8,128)(2,1)}), bf16[2,1024,1152]{2,1,0:T(8,128)(2,1)}) %all-gather.6.cloned.1.call-update) | async-done | bytes 4718608 | tf_op jit(solution)/shard_map/all_gather | solution.py:59
  206.4 5.1 fusion.19
  211.5 2.9 fusion.21
  214.4 29.5 %all-gather.8.cloned.1.call-done = bf16[1152,1024]{1,0:T(8,128)(2,1)} async-done(((bf16[1152,512]{1,0:T(8,128)(2,1)}), bf16[1152,1024]{1,0:T(8,128)(2,1)}) %all-gather.8.cloned.1.call-update) | async-done | bytes 2359312 | tf_op jit(solution)/shard_map/all_gather | solution.py:60
  243.9 6.7 multiply_convert_fusion
  250.6 4.1 fusion.18
  254.6 4.5 fusion.22
  259.4 4.9 fusion.62
  264.3 81.2 %all-reduce.9.cloned.1.call-done = f32[512,1024]{1,0:T(8,128)} async-done(((f32[512,1024]{1,0:T(8,128)}), f32[512,1024]{1,0:T(8,128)}) %all-reduce.9.cloned.1.call-update) | async-done | bytes 2097168 | tf_op jit(solution)/shard_map/psum | solution.py:101
  345.5 2.3 multiply_reduce_fusion
  351.5 1.4 collective-permute-start.1
  353.4 1.3 collective-permute-done.1
  356.3 1.8 add_add_fusion
  358.2 3.2 fusion.38
  361.4 1.6 convolution_bitcast_fusion.3
  364.7 1.8 pad_maximum_fusion.1
  366.6 5.2 fusion.24
  371.8 3.3 convolution_bitcast_fusion
  375.2 1.6 convolution_bitcast_fusion.1
  376.7 4.3 pad_maximum_fusion
  381.3 131.5 %all-reduce.11.cloned.1.call-done = (f32[512,1024]{1,0:T(8,128)}, f32[512,1024]{1,0:T(8,128)}) async-done(((f32[512,1024]{1,0:T(8,128)}, f32[512,1024]{1,0:T(8,128)}), (f32[512,1024]{1,0:T(8,128)}, f32[512,1024]{1,0:T(8,128)})) %all-reduce.11.cloned.1.call-update) | async-done | bytes 4194320 | tf_op jit(solution)/shard_map/psum | solution.py:87
  512.8 2.2 fusion.14
  515.1 1.0 copy.17
  516.2 18.3 %reduce-scatter.10.cloned.1.call-done = f32[256,512]{1,0:T(8,128)} async-done(((f32[256,1024]{1,0:T(8,128)}), f32[256,512]{1,0:T(8,128)}) %reduce-scatter.10.cloned.1.call-update) | async-done | bytes 524304 | tf_op jit(solution)/shard_map/reduce_scatter | solution.py:147
  534.4 45.7 %reduce-scatter.8.cloned.1.call-done = f32[3,512,256]{2,1,0:T(8,128)} async-done(((f32[3,1024,256]{2,1,0:T(8,128)}), f32[3,512,256]{2,1,0:T(8,128)}) %reduce-scatter.8.cloned.1.call-update) | async-done | bytes 1572880 | tf_op jit(solution)/shard_map/reduce_scatter | solution.py:146
  580.1 63.0 %reduce-scatter.14.cloned.1.call-done = f32[1152,512]{1,0:T(8,128)} async-done(((f32[1152,1024]{1,0:T(8,128)}), f32[1152,512]{1,0:T(8,128)}) %reduce-scatter.14.cloned.1.call-update) | async-done | bytes 2359312 | tf_op jit(solution)/shard_map/reduce_scatter | solution.py:149
  643.1 112.8 %reduce-scatter.12.cloned.1.call-done = f32[2,512,1152]{2,1,0:T(8,128)} async-done(((f32[2,1024,1152]{2,1,0:T(8,128)}), f32[2,512,1152]{2,1,0:T(8,128)}) %reduce-scatter.12.cloned.1.call-update) | async-done | bytes 4718608 | tf_op jit(solution)/shard_map/reduce_scatter | solution.py:148
  756.0 13.1 %psum.79 = f32[3,256]{1,0:T(4,128)} all-reduce(f32[3,256]{1,0:T(4,128)S(1)} %pad_maximum_fusion.5), channel_id=1, replica_groups=mesh['fsdp'=2,'context'=4,'tensor'=4] {'fsdp','context'}, use_global_device_ids=true, to_apply=%region_25.26 | all-reduce | flops 768 | bytes 6144 | tf_op jit(solution)/shard_map/psum | solution.py:153
  769.1 3.6 add_bitcast_fusion
  772.8 1.9 fusion.12
  774.7 1.1 copy.18
  775.8 6.3 psum.78
  782.1 159.7 %all-reduce.13.cloned.1.call-done = (f32[3,512,256]{2,1,0:T(8,128)}, f32[256,512]{1,0:T(8,128)}, f32[2,512,1152]{2,1,0:T(8,128)}, f32[1152,512]{1,0:T(8,128)}) async-done(((f32[3,512,256]{2,1,0:T(8,128)}, f32[256,512]{1,0:T(8,128)}, f32[2,512,1152]{2,1,0:T(8,128)}, f32[1152,512]{1,0:T(8,128)}), (f32[3,512,256]{2,1,0:T(8,128)}, f32[256,512]{1,0:T(8,128)}, f32[2,512,1152]{2,1,0:T(8,128)}, ...) | async-done | bytes 9175056 | tf_op jit(solution)/shard_map/psum | solution.py:152
  941.8 2.7 copy.27
  945.3 5.0 copy.29
  950.3 1.4 copy.30
  (112 shorter events, 14.2 us)
Async XLA Ops:
  7.2 32.3 %all-gather.4.cloned.1.call-start = ((), (), s32[]{:S(2)}) async-start(), calls=%async_computation.5 | async-start | bytes 2359296 | tf_op jit(solution)/shard_map/all_gather | solution.py:57
  7.9 135.3 %all-reduce.7.cloned.1.call-start = ((), (), s32[]{:S(2)}) async-start(), calls=%async_computation.6 | async-start | bytes 4194304 | tf_op jit(solution)/shard_map/psum | solution.py:79
  15.0 26.4 %copy-start.2 = (bf16[1,512,1024]{2,1,0:T(8,128)(2,1)S(1)}, bf16[1,512,1024]{2,1,0:T(8,128)(2,1)}, u32[]{:S(2)}) copy-start(bf16[1,512,1024]{2,1,0:T(8,128)(2,1)} %param.9) | copy-start | bytes 3145732
  39.5 2.0 copy-start.11
  41.5 1.3 copy-start.23
  41.5 2.9 copy-start.28
  42.8 12.1 %copy-start.20 = (f32[512,256]{1,0:T(8,128)}, f32[512,256]{1,0:T(8,128)S(1)}, u32[]{:S(2)}) copy-start(f32[512,256]{1,0:T(8,128)S(1)} %get-tuple-element.43) | copy-start | bytes 1572868
  42.8 10.5 %collective-permute-start = (f32[2,256]{1,0:T(2,128)S(1)}, f32[2,256]{1,0:T(2,128)S(1)}, u32[]{:S(2)}, u32[]{:S(2)}) collective-permute-start(f32[2,256]{1,0:T(2,128)S(1)} %slice.98), channel_id=1, source_target_pairs={{0,4},{4,8},{8,12},{1,5},{5,9},{9,13},{2,6},{6,10},{10,14},{3,7},{... | collective-permute-start | bytes 6152 | tf_op jit(solution)/shard_map/ppermute | solution.py:12
  53.3 1.6 copy-start.7
  54.9 0.7 copy-start.18
  57.3 149.1 %all-gather.6.cloned.1.call-start = ((), (), s32[]{:S(2)}) async-start(), calls=%async_computation.7 | async-start | bytes 7077888 | tf_op jit(solution)/shard_map/all_gather | solution.py:59
  58.1 185.8 %all-gather.8.cloned.1.call-start = ((), (), s32[]{:S(2)}) async-start(), calls=%async_computation.8 | async-start | bytes 3538944 | tf_op jit(solution)/shard_map/all_gather | solution.py:60
  58.7 286.9 %all-reduce.9.cloned.1.call-start = ((), (), s32[]{:S(2)}) async-start(), calls=%async_computation.9 | async-start | bytes 4194304 | tf_op jit(solution)/shard_map/psum | solution.py:101
  206.4 5.1 copy-start.3
  206.4 5.1 copy-start.29
  250.5 4.1 copy-start.13
  250.5 4.1 copy-start.15
  259.2 253.6 %all-reduce.11.cloned.1.call-start = ((), (), s32[]{:S(2)}) async-start(), calls=%async_computation.15 | async-start | bytes 8388608 | tf_op jit(solution)/shard_map/psum | solution.py:87
  345.5 2.3 copy-start.5
  345.5 2.5 copy-start.9
  348.0 1.0 copy-start.8
  349.1 2.4 copy-start
  349.1 1.4 copy-start.21
  349.1 2.0 copy-start.26
  349.1 2.1 copy-start.27
  349.6 3.4 copy-start.12
  351.5 3.5 copy-start.19
  351.5 3.2 copy-start.22
  351.5 3.2 collective-permute-start.1
  353.0 2.0 copy-start.24
  355.1 0.7 copy-start.16
  358.1 176.3 %reduce-scatter.10.cloned.1.call-start = ((), (), s32[]{:S(2)}) async-start(), calls=%async_computation.11 | async-start | bytes 1572864 | tf_op jit(solution)/shard_map/reduce_scatter | solution.py:147
  361.4 218.7 %reduce-scatter.8.cloned.1.call-start = ((), (), s32[]{:S(2)}) async-start(), calls=%async_computation.10 | async-start | bytes 4718592 | tf_op jit(solution)/shard_map/reduce_scatter | solution.py:146
  363.0 1.0 copy-start.17
  366.5 276.6 %reduce-scatter.14.cloned.1.call-start = ((), (), s32[]{:S(2)}) async-start(), calls=%async_computation.13 | async-start | bytes 7077888 | tf_op jit(solution)/shard_map/reduce_scatter | solution.py:149
  371.8 384.2 %reduce-scatter.12.cloned.1.call-start = ((), (), s32[]{:S(2)}) async-start(), calls=%async_computation.12 | async-start | bytes 14155776 | tf_op jit(solution)/shard_map/reduce_scatter | solution.py:148
  371.8 3.3 copy-start.4
  371.8 3.3 copy-start.14
  381.0 393.7 %reduce-scatter.16.cloned.1.call-start = ((), (), s32[]{:S(2)}) async-start(), calls=%async_computation.14 | async-start | bytes 786432
  516.1 425.7 %all-reduce.13.cloned.1.call-start = ((), (), s32[]{:S(2)}) async-start(), calls=%async_computation.16 | async-start | bytes 18350080 | tf_op jit(solution)/shard_map/psum | solution.py:152
  769.1 3.6 copy-start.1
  769.1 3.6 copy-start.6
  941.8 2.7 copy-start.25
  945.3 5.0 copy-start.10
Sparse Core Ops, SparseCore 0:
  9.5 29.8 all-gather.3
  57.5 85.6 all-reduce.6
  144.7 61.6 all-gather.5
  207.8 36.0 all-gather.7
  259.3 86.1 all-reduce.8
  358.2 154.5 all-reduce.10
  515.0 19.3 reduce-scatter.9
  536.7 43.3 reduce-scatter.7
  583.0 60.0 reduce-scatter.13
  645.3 110.6 reduce-scatter.11
  758.8 14.6 reduce-scatter.15
  776.1 165.6 all-reduce.12
where the time goes:
time: 959 us
  waiting for transfers between devices  811 us (85%)
  matrix products  54 us (6%)
  blocking collectives  33.8 us (4%)
  other arithmetic  23.9 us (2%)
  local copies, waits for them, and re-layouts  17 us (2%)
  between operations  14.6 us (2%)
    psum x1, waiting for transfers between devices, local(): lax.psum((pieces[0], pieces[1], pieces[2], pieces[3], pieces[4]), 'context')  160 us
    psum x1, waiting for transfers between devices, local(): lax.psum(matmul_plain(act_value, full_down), 'tensor')  131 us
    reduce_scatter x1, waiting for transfers between devices, local(): lax.psum_scatter(term_gate_up, 'fsdp', scatter_dimension=1, tiled=True)  113 us
    psum x1, waiting for transfers between devices, local(): first_sum = inputs + lax.psum(matmul_plain(gated, full_out), 'tensor')  84.5 us
    psum x1, waiting for transfers between devices, local(): lax.psum(matmul_right(grad_gate, full_gate_up[0]) + matmul_right(grad_up,...  81.2 us
    reduce_scatter x1, waiting for transfers between devices, local(): lax.psum_scatter(term_down, 'fsdp', scatter_dimension=1, tiled=True)  63 us
    all_gather x1, waiting for transfers between devices, local(): lax.all_gather(w_gate_up, 'fsdp', axis=1, tiled=True)  60 us
    reduce_scatter x1, waiting for transfers between devices, local(): lax.psum_scatter(term_in, 'fsdp', scatter_dimension=1, tiled=True)  45.7 us
  transfers between devices with their start and end apart: 14, of which 12 were waited for; matrix products, arithmetic and copies ran while one was open for 5% of the time, Pallas kernels for 0%

commit v1 on v0

--- a/solution.py
+++ b/solution.py
@@ -4,6 +4,27 @@
 from jax.sharding import PartitionSpec as P
 
 norm_eps = 1e-05
+
+
+def joined_along(tiles, dim):
+    shape = list(tiles.shape[1:])
+    shape[dim] *= tiles.shape[0]
+    return jnp.moveaxis(tiles, 0, dim).reshape(shape)
+
+
+def doubled(x, axis):
+    peers, place = (lax.axis_size(axis), lax.axis_index(axis))
+    blocks, bit = (x[None], 1)
+    while bit < peers:
+        other = lax.ppermute(blocks, axis, [(i, i ^ bit) for i in range(peers)])
+        low = place & bit == 0
+        blocks = jnp.concatenate([jnp.where(low, blocks, other), jnp.where(low, other, blocks)])
+        bit *= 2
+    return blocks
+
+
+def collect(shard, axis, dim):
+    return joined_along(doubled(shard, axis), dim)
 
 
 def shifted(block, axis, distance):
@@ -56,7 +77,7 @@
     full_in, full_out, full_gate_up, full_down, full_gains = (
         lax.all_gather(w_in, "fsdp", axis=1, tiled=True),
         lax.all_gather(w_out, "fsdp", axis=1, tiled=True),
-        lax.all_gather(w_gate_up, "fsdp", axis=1, tiled=True),
+        collect(w_gate_up, "fsdp", 1),
         lax.all_gather(w_down, "fsdp", axis=1, tiled=True),
         lax.all_gather(norm_gains, "fsdp", axis=1, tiled=True),
     )

time: 959 us -> 955 us (level)
    psum x1, waiting for transfers between devices: 84.5 us -> 51.3 us  [local(): first_sum = inputs + lax.psum(matmul_plain(gated, full_out), 'tensor')]
    ppermute x0 -> x1, waiting for transfers between devices: none -> 28.8 us  [doubled(): other = lax.ppermute(blocks, axis, [(i, i ^ bit) for i in range(peers)])]
  transfers between devices with their start and end apart: 14 -> 15, of which waited for: 12 -> 13; matrix products, arithmetic and copies ran while one was open for 5% -> 7% of each run, Pallas kernels for 0% -> 0%
where the time goes in v1:
time: 955 us
  waiting for transfers between devices  807 us (85%)
  matrix products  47.5 us (5%)
  blocking collectives  35 us (4%)
  other arithmetic  24.1 us (3%)
  local copies, waits for them, and re-layouts  21.5 us (2%)
  between operations  14.7 us (2%)
    psum x1, waiting for transfers between devices, local(): lax.psum((pieces[0], pieces[1], pieces[2], pieces[3], pieces[4]), 'context')  160 us
    psum x1, waiting for transfers between devices, local(): lax.psum(matmul_plain(act_value, full_down), 'tensor')  132 us
    reduce_scatter x1, waiting for transfers between devices, local(): lax.psum_scatter(term_gate_up, 'fsdp', scatter_dimension=1, tiled=True)  113 us
    psum x1, waiting for transfers between devices, local(): lax.psum(matmul_right(grad_gate, full_gate_up[0]) + matmul_right(grad_up,...  81.2 us
    reduce_scatter x1, waiting for transfers between devices, local(): lax.psum_scatter(term_down, 'fsdp', scatter_dimension=1, tiled=True)  63 us
    all_gather x1, waiting for transfers between devices, local(): lax.all_gather(w_gate_up, 'fsdp', axis=1, tiled=True)  52.5 us
    psum x1, waiting for transfers between devices, local(): first_sum = inputs + lax.psum(matmul_plain(gated, full_out), 'tensor')  51.3 us
    reduce_scatter x1, waiting for transfers between devices, local(): lax.psum_scatter(term_in, 'fsdp', scatter_dimension=1, tiled=True)  45.7 us
  transfers between devices with their start and end apart: 15, of which 13 were waited for; matrix products, arithmetic and copies ran while one was open for 7% of the time, Pallas kernels for 0%

profile of v1, /device:TPU:0, one launch (start us, length us, event | category | flops | bytes accessed | tf_op | source)
XLA Modules:
  0.0 954.8 jit_solution(4934432955511233261)
XLA Ops:
  10.5 5.3 all_gather.18
  16.0 23.4 %all-gather.4.cloned.1.call-done = bf16[3,1024,256]{2,1,0:T(8,128)(2,1)} async-done(((bf16[3,512,256]{2,1,0:T(8,128)(2,1)}), bf16[3,1024,256]{2,1,0:T(8,128)(2,1)}) %all-gather.4.cloned.1.call-update) | async-done | bytes 1572880 | tf_op jit(solution)/shard_map/all_gather | solution.py:78
  39.5 1.6 fusion.44
  41.2 1.3 fusion.59
  42.5 1.6 collective-permute-start
  44.1 10.2 %all_gather.20 = bf16[256,1024]{1,0:T(8,128)(2,1)S(1)} all-gather(bf16[256,512]{1,0:T(8,128)(2,1)S(1)} %copy-done.31), channel_id=1, replica_groups=mesh['fsdp'=2,'context'=4,'tensor'=4] {'fsdp'}, dimensions={1}, use_global_device_ids=true | all-gather | bytes 786432 | tf_op jit(solution)/shard_map/all_gather | solution.py:79
  54.3 1.6 multiply_convert_fusion.7
  56.6 1.8 fusion.60
  59.3 36.4 %all-gather.6.cloned.1.call-done = bf16[1152,1024]{1,0:T(8,128)(2,1)} async-done(((bf16[1152,512]{1,0:T(8,128)(2,1)}), bf16[1152,1024]{1,0:T(8,128)(2,1)}) %all-gather.6.cloned.1.call-update) | async-done | bytes 2359312 | tf_op jit(solution)/shard_map/all_gather | solution.py:81
  95.6 4.8 fusion.24
  100.4 28.8 %collective-permute-done.1 = bf16[1,2,512,1152]{3,2,1,0:T(8,128)(2,1)} collective-permute-done((bf16[1,2,512,1152]{3,2,1,0:T(8,128)(2,1)}, bf16[1,2,512,1152]{3,2,1,0:T(8,128)(2,1)}, u32[]{:S(2)}, u32[]{:S(2)}) %collective-permute-start.1) | collective-permute-done | bytes 2359328 | tf_op jit(solution)/shard_map/ppermute | solution.py:19
  129.2 2.1 broadcast_select_fusion.1
  131.8 2.6 fusion.55
  134.4 51.3 %all-reduce.7.cloned.1.call-done = f32[512,1024]{1,0:T(8,128)} async-done(((f32[512,1024]{1,0:T(8,128)}), f32[512,1024]{1,0:T(8,128)}) %all-reduce.7.cloned.1.call-update) | async-done | bytes 2097168 | tf_op jit(solution)/shard_map/psum | solution.py:100
  185.7 1.9 multiply_reduce_fusion.2
  187.9 1.8 copy-done.14
  189.7 1.5 fusion.61
  192.1 4.2 multiply_convert_fusion.1
  196.3 52.5 %all-gather.8.cloned.1.call-done = bf16[2,1024,1152]{2,1,0:T(8,128)(2,1)} async-done(((bf16[2,512,1152]{2,1,0:T(8,128)(2,1)}), bf16[2,1024,1152]{2,1,0:T(8,128)(2,1)}) %all-gather.8.cloned.1.call-update) | async-done | bytes 4718608 | tf_op jit(solution)/shard_map/all_gather | solution.py:112
  248.8 3.7 fusion.7
  252.6 2.9 fusion.20
  255.7 4.9 fusion.62
  260.6 81.2 %all-reduce.9.cloned.1.call-done = f32[512,1024]{1,0:T(8,128)} async-done(((f32[512,1024]{1,0:T(8,128)}), f32[512,1024]{1,0:T(8,128)}) %all-reduce.9.cloned.1.call-update) | async-done | bytes 2097168 | tf_op jit(solution)/shard_map/psum | solution.py:122
  341.8 2.3 multiply_reduce_fusion
  347.8 1.4 collective-permute-start.2
  349.7 1.3 collective-permute-done.2
  352.5 1.8 add_add_fusion
  354.4 3.1 fusion.36
  357.6 1.6 convolution_bitcast_fusion.3
  360.8 1.8 pad_maximum_fusion.1
  362.7 5.2 fusion.22
  368.0 3.3 convolution_bitcast_fusion
  371.3 1.6 convolution_bitcast_fusion.1
  372.9 4.3 pad_maximum_fusion
  377.5 131.6 %all-reduce.11.cloned.1.call-done = (f32[512,1024]{1,0:T(8,128)}, f32[512,1024]{1,0:T(8,128)}) async-done(((f32[512,1024]{1,0:T(8,128)}, f32[512,1024]{1,0:T(8,128)}), (f32[512,1024]{1,0:T(8,128)}, f32[512,1024]{1,0:T(8,128)})) %all-reduce.11.cloned.1.call-update) | async-done | bytes 4194320 | tf_op jit(solution)/shard_map/psum | solution.py:108
  509.1 2.2 fusion.16
  512.4 18.3 %reduce-scatter.10.cloned.1.call-done = f32[256,512]{1,0:T(8,128)} async-done(((f32[256,1024]{1,0:T(8,128)}), f32[256,512]{1,0:T(8,128)}) %reduce-scatter.10.cloned.1.call-update) | async-done | bytes 524304 | tf_op jit(solution)/shard_map/reduce_scatter | solution.py:168
  530.7 45.7 %reduce-scatter.8.cloned.1.call-done = f32[3,512,256]{2,1,0:T(8,128)} async-done(((f32[3,1024,256]{2,1,0:T(8,128)}), f32[3,512,256]{2,1,0:T(8,128)}) %reduce-scatter.8.cloned.1.call-update) | async-done | bytes 1572880 | tf_op jit(solution)/shard_map/reduce_scatter | solution.py:167
  576.4 63.0 %reduce-scatter.14.cloned.1.call-done = f32[1152,512]{1,0:T(8,128)} async-done(((f32[1152,1024]{1,0:T(8,128)}), f32[1152,512]{1,0:T(8,128)}) %reduce-scatter.14.cloned.1.call-update) | async-done | bytes 2359312 | tf_op jit(solution)/shard_map/reduce_scatter | solution.py:170
  639.4 112.8 %reduce-scatter.12.cloned.1.call-done = f32[2,512,1152]{2,1,0:T(8,128)} async-done(((f32[2,1024,1152]{2,1,0:T(8,128)}), f32[2,512,1152]{2,1,0:T(8,128)}) %reduce-scatter.12.cloned.1.call-update) | async-done | bytes 4718608 | tf_op jit(solution)/shard_map/reduce_scatter | solution.py:169
  752.2 13.1 %psum.79 = f32[3,256]{1,0:T(4,128)} all-reduce(f32[3,256]{1,0:T(4,128)S(1)} %pad_maximum_fusion.5), channel_id=1, replica_groups=mesh['fsdp'=2,'context'=4,'tensor'=4] {'fsdp','context'}, use_global_device_ids=true, to_apply=%region_25.26 | all-reduce | flops 768 | bytes 6144 | tf_op jit(solution)/shard_map/psum | solution.py:174
  765.4 3.6 add_bitcast_fusion
  769.0 1.9 fusion.14
  772.0 6.3 psum.78
  778.3 159.7 %all-reduce.13.cloned.1.call-done = (f32[3,512,256]{2,1,0:T(8,128)}, f32[256,512]{1,0:T(8,128)}, f32[2,512,1152]{2,1,0:T(8,128)}, f32[1152,512]{1,0:T(8,128)}) async-done(((f32[3,512,256]{2,1,0:T(8,128)}, f32[256,512]{1,0:T(8,128)}, f32[2,512,1152]{2,1,0:T(8,128)}, f32[1152,512]{1,0:T(8,128)}), (f32[3,512,256]{2,1,0:T(8,128)}, f32[256,512]{1,0:T(8,128)}, f32[2,512,1152]{2,1,0:T(8,128)}, ...) | async-done | bytes 9175056 | tf_op jit(solution)/shard_map/psum | solution.py:173
  938.1 2.7 copy.27
  941.6 5.0 copy.29
  946.6 1.4 copy.30
  (129 shorter events, 17.7 us)
Async XLA Ops:
  7.2 3.1 copy-start.2
  7.2 3.3 copy-start.33
  7.2 8.7 copy-start.32
  7.2 32.3 %all-gather.4.cloned.1.call-start = ((), (), s32[]{:S(2)}) async-start(), calls=%async_computation.5 | async-start | bytes 2359296 | tf_op jit(solution)/shard_map/all_gather | solution.py:78
  7.9 87.7 %all-gather.6.cloned.1.call-start = ((), (), s32[]{:S(2)}) async-start(), calls=%async_computation.7 | async-start | bytes 3538944 | tf_op jit(solution)/shard_map/all_gather | solution.py:81
  8.7 177.0 %all-reduce.7.cloned.1.call-start = ((), (), s32[]{:S(2)}) async-start(), calls=%async_computation.6 | async-start | bytes 4194304 | tf_op jit(solution)/shard_map/psum | solution.py:100
  39.5 1.7 copy-start.15
  41.2 1.3 copy-start.26
  41.2 2.9 copy-start.31
  42.5 13.4 %copy-start.23 = (f32[512,256]{1,0:T(8,128)}, f32[512,256]{1,0:T(8,128)S(1)}, u32[]{:S(2)}) copy-start(f32[512,256]{1,0:T(8,128)S(1)} %get-tuple-element.47) | copy-start | bytes 1572868
  42.5 11.8 %collective-permute-start = (f32[2,256]{1,0:T(2,128)S(1)}, f32[2,256]{1,0:T(2,128)S(1)}, u32[]{:S(2)}, u32[]{:S(2)}) collective-permute-start(f32[2,256]{1,0:T(2,128)S(1)} %slice.106), channel_id=1, source_target_pairs={{0,4},{4,8},{8,12},{1,5},{5,9},{9,13},{2,6},{6,10},{10,14},{3,7},{... | collective-permute-start | bytes 6152 | tf_op jit(solution)/shard_map/ppermute | solution.py:33
  54.3 1.6 copy-start.8
  58.4 37.3 %copy-start.10 = (bf16[1,512,1024]{2,1,0:T(8,128)(2,1)S(1)}, bf16[1,512,1024]{2,1,0:T(8,128)(2,1)}, u32[]{:S(2)}) copy-start(bf16[1,512,1024]{2,1,0:T(8,128)(2,1)} %param.10) | copy-start | bytes 3145732
  58.4 190.4 %all-gather.8.cloned.1.call-start = ((), (), s32[]{:S(2)}) async-start(), calls=%async_computation.8 | async-start | bytes 7077888 | tf_op jit(solution)/shard_map/all_gather | solution.py:112
  58.4 70.8 %collective-permute-start.1 = (bf16[1,2,512,1152]{3,2,1,0:T(8,128)(2,1)}, bf16[1,2,512,1152]{3,2,1,0:T(8,128)(2,1)}, u32[]{:S(2)}, u32[]{:S(2)}) collective-permute-start(bf16[1,2,512,1152]{3,2,1,0:T(8,128)(2,1)} %bitcast.134), channel_id=1, source_target_pairs={{0,16},{16,0},{1,17},{17,1},{2,18},{18,2},{3,19},{19,3},{4,20},{20... | collective-permute-start | bytes 7077896 | tf_op jit(solution)/shard_map/ppermute | solution.py:19
  59.2 282.5 %all-reduce.9.cloned.1.call-start = ((), (), s32[]{:S(2)}) async-start(), calls=%async_computation.9 | async-start | bytes 4194304 | tf_op jit(solution)/shard_map/psum | solution.py:122
  95.6 33.6 %copy-start.3 = (bf16[2,512,1152]{2,1,0:T(8,128)(2,1)S(1)}, bf16[2,512,1152]{2,1,0:T(8,128)(2,1)}, u32[]{:S(2)}) copy-start(bf16[2,512,1152]{2,1,0:T(8,128)(2,1)} %param.14) | copy-start | bytes 7077892
  187.6 2.0 copy-start.14
  187.9 3.3 copy-start.4
  189.7 1.7 copy-start.13
  189.7 2.4 copy-start.35
  248.8 3.7 copy-start.17
  248.8 3.8 copy-start.34
  255.5 253.6 %all-reduce.11.cloned.1.call-start = ((), (), s32[]{:S(2)}) async-start(), calls=%async_computation.15 | async-start | bytes 8388608 | tf_op jit(solution)/shard_map/psum | solution.py:108
  341.8 2.3 copy-start.6
  341.8 2.5 copy-start.11
  344.3 1.0 copy-start.9
  345.3 2.4 copy-start
  345.3 1.4 copy-start.24
  345.3 2.0 copy-start.29
  345.3 2.1 copy-start.30
  345.8 3.4 copy-start.16
  347.7 3.5 copy-start.22
  347.7 3.2 copy-start.25
  347.8 3.2 collective-permute-start.2
  349.2 2.0 copy-start.27
  354.4 176.3 %reduce-scatter.10.cloned.1.call-start = ((), (), s32[]{:S(2)}) async-start(), calls=%async_computation.11 | async-start | bytes 1572864 | tf_op jit(solution)/shard_map/reduce_scatter | solution.py:168
  357.6 218.8 %reduce-scatter.8.cloned.1.call-start = ((), (), s32[]{:S(2)}) async-start(), calls=%async_computation.10 | async-start | bytes 4718592 | tf_op jit(solution)/shard_map/reduce_scatter | solution.py:167
  362.7 276.7 %reduce-scatter.14.cloned.1.call-start = ((), (), s32[]{:S(2)}) async-start(), calls=%async_computation.13 | async-start | bytes 7077888 | tf_op jit(solution)/shard_map/reduce_scatter | solution.py:170
  367.9 384.3 %reduce-scatter.12.cloned.1.call-start = ((), (), s32[]{:S(2)}) async-start(), calls=%async_computation.12 | async-start | bytes 14155776 | tf_op jit(solution)/shard_map/reduce_scatter | solution.py:169
  368.0 3.3 copy-start.5
  368.0 3.3 copy-start.18
  377.2 393.7 %reduce-scatter.16.cloned.1.call-start = ((), (), s32[]{:S(2)}) async-start(), calls=%async_computation.14 | async-start | bytes 786432
  512.4 425.7 %all-reduce.13.cloned.1.call-start = ((), (), s32[]{:S(2)}) async-start(), calls=%async_computation.16 | async-start | bytes 18350080 | tf_op jit(solution)/shard_map/psum | solution.py:173
  765.4 3.6 copy-start.1
  765.4 3.6 copy-start.7
  938.1 2.7 copy-start.28
  941.6 5.0 copy-start.12
  (3 other events, 2.4 us)
Sparse Core Ops, SparseCore 0:
  9.5 29.8 all-gather.3
  41.0 54.5 all-gather.5
  98.6 87.0 all-reduce.6
  187.1 61.6 all-gather.7
  255.6 86.1 all-reduce.8
  354.5 154.5 all-reduce.10
  511.3 19.3 reduce-scatter.9
  532.9 43.3 reduce-scatter.7
  579.3 60.0 reduce-scatter.13
  641.5 110.6 reduce-scatter.11
  755.0 14.6 reduce-scatter.15
  772.4 165.6 all-reduce.12
